TPU v7x, 32 devices: a whole 2x2x4 slice. The times are simulated.
32 devices in a mesh: state: 8 (over y, x, core), dp: 4 (over z).
Axes of the slice: x: 2, y: 2, z: 4, core: 2. Of those that a mesh axis runs over, the one named last changes fastest.
Arguments:
- state_ensemble: float32 [16384, 256], P('state'), may hold values from -80 to 80, as said below
- predicted_data: float32 [16384, 256], P(('state', 'dp')), may hold values from -125 to 125, as said below
- innovations: bfloat16 [16384, 256], P(('state', 'dp')), may hold values from -6 to 6
Outputs:
- increment: float32 [16384, 256], P(('state', 'dp'))
Inputs may be any that keep to these rules, and one draw needn't show every extreme that they name: `state_ensemble`: finite values. `predicted_data`: finite values.
All inputs are finite; a program needn't handle non-finite values.
Results may differ from a plain program's by a relative error of at most 0.0042.
Values may be sent and summed in bfloat16 or wider, within the bound.
A program may use at most 64 MiB of HBM per device.

v0:
```python
import math

import jax
import jax.numpy as jnp
from jax import lax
from jax.sharding import PartitionSpec as P


def standardize(values):
    members = values.shape[1]
    anomalies = values - jnp.mean(values, axis=1, keepdims=True)
    spread = jnp.sqrt(jnp.sum(anomalies * anomalies, axis=1) / (members - 1) + 1e-06)
    return ((anomalies / spread[:, None]).astype(jnp.bfloat16), spread)


def add_block(running, state_std, data_part, innov_part):
    members = state_std.shape[1]
    count = data_part.shape[0]
    block_size = math.gcd(count, 512)
    data_blocks = data_part.reshape(count // block_size, block_size, members)
    innov_blocks = innov_part.reshape(count // block_size, block_size, members)

    def advance(partial_sum, pair):
        correl = lax.dot_general(
            state_std, pair[0], (((1,), (1,)), ((), ())), preferred_element_type=jnp.float32
        ) / (members - 1)
        localized = (correl * correl * correl).astype(jnp.bfloat16)
        return (partial_sum + jnp.dot(localized, pair[1], preferred_element_type=jnp.float32), None)

    return lax.scan(advance, running, (data_blocks, innov_blocks))[0]


def on_device(state_ensemble, predicted_data, innovations):
    state_std, spread = standardize(state_ensemble)
    data_std, unused = standardize(predicted_data)
    start_zero = jnp.zeros(state_ensemble.shape, jnp.float32)
    summed = add_block(
        start_zero,
        state_std,
        lax.all_gather(data_std, "state", axis=0, tiled=True),
        lax.all_gather(innovations, "state", axis=0, tiled=True),
    )
    row_count = state_ensemble.shape[0] // lax.axis_size("dp")
    first_row = lax.axis_index("dp") * row_count
    own_spread = lax.dynamic_slice_in_dim(spread, first_row, row_count, 0)
    own_rows = lax.psum_scatter(summed, "dp", scatter_dimension=0, tiled=True)
    return own_spread[:, None] * own_rows


def solution(mesh):
    in_specs = (P("state", None), P(("state", "dp"), None), P(("state", "dp"), None))
    out_specs = P(("state", "dp"), None)
    return jax.shard_map(
        on_device, mesh=mesh, in_specs=in_specs, out_specs=out_specs, check_vma=False
    )
```

profile of v0, /device:TPU:1, one launch (start us, length us, event | category | flops | bytes accessed | tf_op | source)
XLA Modules:
  0.0 155.2 jit_solution(8157323247590188585)
XLA Ops:
  6.5 0.7 all-gather.5.cloned.1.call-update
  7.3 0.0 all-gather.3.cloned.1.call-start
  7.3 1.2 reduce_sum.38
  8.5 1.3 multiply_reduce_fusion.1
  9.8 2.0 %divide_convert_fusion.1 = bf16[512,256]{1,0:T(8,128)(2,1)} fusion(f32[512,256]{1,0:T(8,128)} %param.6, f32[512]{0:T(512)S(1)} %add_sqrt_fusion.1, f32[512]{0:T(512)S(1)} %broadcast_multiply_fusion.2), kind=kLoop, calls=%fused_computation.11 | loop fusion | flops 393216 | bytes 790528 | tf_op jit(solution)/shard_map/convert_element_type | solution.py:13
  11.8 0.0 all-gather.3.cloned.1.call-update
  11.8 0.0 reduce-scatter.2.cloned.1.call-start
  11.8 0.3 reduce_sum.36
  12.2 0.6 multiply_reduce_fusion
  12.9 0.7 divide_convert_fusion
  13.6 25.9 %all-gather.5.cloned.1.call-done = bf16[4096,256]{1,0:T(8,128)(2,1)} async-done(((bf16[512,256]{1,0:T(8,128)(2,1)}), bf16[4096,256]{1,0:T(8,128)(2,1)}) %all-gather.5.cloned.1.call-update) | async-done | bytes 2097168 | tf_op jit(solution)/shard_map/all_gather | solution.py:41
  39.5 29.7 %all-gather.3.cloned.1.call-done = bf16[4096,256]{1,0:T(8,128)(2,1)} async-done(((bf16[512,256]{1,0:T(8,128)(2,1)}), bf16[4096,256]{1,0:T(8,128)(2,1)}) %all-gather.3.cloned.1.call-update) | async-done | bytes 2097168 | tf_op jit(solution)/shard_map/all_gather | solution.py:40
  69.2 34.6 %while.11 = (s32[]{:T(128)}, f32[2048,256]{1,0:T(8,128)}, bf16[8,512,256]{2,1,0:T(8,128)(2,1)}, bf16[2048,256]{1,0:T(8,128)(2,1)S(1)}, bf16[8,512,256]{2,1,0:T(8,128)(2,1)}, /*index=5*/s32[]{:T(128)}, s32[]{:T(128)}) while((s32[]{:T(128)}, f32[2048,256]{1,0:T(8,128)}, bf16[8,512,256]{2,1,0:T(8,128)(2,1)}, ...), condition=%wide.region_5.6_spmd.clone, body=%wide.region_4.5_spmd.clone.sunk | while | flops 1078984704 | bytes 5768798 | solution.py:30
  69.2 3.7 %convolution_add_fusion.2 = f32[2048,256]{1,0:T(8,128)} fusion(f32[2048,256]{1,0:T(8,128)} %get-tuple-element.100, bf16[2048,256]{1,0:T(8,128)(2,1)S(1)} %get-tuple-element.109, pred[]{:T(512)S(6)} %compare.3, bf16[8,512,256]{2,1,0:T(8,128)(2,1)} %get-tuple-element.110, s32[]{:T(128)S(6)} %copy.6, bf16[8,512,256]{2,1,0:T(8,128)(2,1)} %get-tuple-element.108), kind=kOutput, calls=%fused_computation.2.clone.1 | convolution fusion | flops 1078984704 | bytes 5768704 | tf_op jit(solution)/shard_map/while/body/eval_jaxpr/dot_general | solution.py:28
  72.9 4.4 %convolution_add_fusion.2 = f32[2048,256]{1,0:T(8,128)} fusion(f32[2048,256]{1,0:T(8,128)} %get-tuple-element.100, bf16[2048,256]{1,0:T(8,128)(2,1)S(1)} %get-tuple-element.109, pred[]{:T(512)S(6)} %compare.3, bf16[8,512,256]{2,1,0:T(8,128)(2,1)} %get-tuple-element.110, s32[]{:T(128)S(6)} %copy.6, bf16[8,512,256]{2,1,0:T(8,128)(2,1)} %get-tuple-element.108), kind=kOutput, calls=%fused_computation.2.clone.1 | convolution fusion | flops 1078984704 | bytes 5768704 | tf_op jit(solution)/shard_map/while/body/eval_jaxpr/dot_general | solution.py:28
  77.3 4.4 %convolution_add_fusion.2 = f32[2048,256]{1,0:T(8,128)} fusion(f32[2048,256]{1,0:T(8,128)} %get-tuple-element.100, bf16[2048,256]{1,0:T(8,128)(2,1)S(1)} %get-tuple-element.109, pred[]{:T(512)S(6)} %compare.3, bf16[8,512,256]{2,1,0:T(8,128)(2,1)} %get-tuple-element.110, s32[]{:T(128)S(6)} %copy.6, bf16[8,512,256]{2,1,0:T(8,128)(2,1)} %get-tuple-element.108), kind=kOutput, calls=%fused_computation.2.clone.1 | convolution fusion | flops 1078984704 | bytes 5768704 | tf_op jit(solution)/shard_map/while/body/eval_jaxpr/dot_general | solution.py:28
  81.7 4.4 %convolution_add_fusion.2 = f32[2048,256]{1,0:T(8,128)} fusion(f32[2048,256]{1,0:T(8,128)} %get-tuple-element.100, bf16[2048,256]{1,0:T(8,128)(2,1)S(1)} %get-tuple-element.109, pred[]{:T(512)S(6)} %compare.3, bf16[8,512,256]{2,1,0:T(8,128)(2,1)} %get-tuple-element.110, s32[]{:T(128)S(6)} %copy.6, bf16[8,512,256]{2,1,0:T(8,128)(2,1)} %get-tuple-element.108), kind=kOutput, calls=%fused_computation.2.clone.1 | convolution fusion | flops 1078984704 | bytes 5768704 | tf_op jit(solution)/shard_map/while/body/eval_jaxpr/dot_general | solution.py:28
  86.1 4.4 %convolution_add_fusion.2 = f32[2048,256]{1,0:T(8,128)} fusion(f32[2048,256]{1,0:T(8,128)} %get-tuple-element.100, bf16[2048,256]{1,0:T(8,128)(2,1)S(1)} %get-tuple-element.109, pred[]{:T(512)S(6)} %compare.3, bf16[8,512,256]{2,1,0:T(8,128)(2,1)} %get-tuple-element.110, s32[]{:T(128)S(6)} %copy.6, bf16[8,512,256]{2,1,0:T(8,128)(2,1)} %get-tuple-element.108), kind=kOutput, calls=%fused_computation.2.clone.1 | convolution fusion | flops 1078984704 | bytes 5768704 | tf_op jit(solution)/shard_map/while/body/eval_jaxpr/dot_general | solution.py:28
  90.5 4.4 %convolution_add_fusion.2 = f32[2048,256]{1,0:T(8,128)} fusion(f32[2048,256]{1,0:T(8,128)} %get-tuple-element.100, bf16[2048,256]{1,0:T(8,128)(2,1)S(1)} %get-tuple-element.109, pred[]{:T(512)S(6)} %compare.3, bf16[8,512,256]{2,1,0:T(8,128)(2,1)} %get-tuple-element.110, s32[]{:T(128)S(6)} %copy.6, bf16[8,512,256]{2,1,0:T(8,128)(2,1)} %get-tuple-element.108), kind=kOutput, calls=%fused_computation.2.clone.1 | convolution fusion | flops 1078984704 | bytes 5768704 | tf_op jit(solution)/shard_map/while/body/eval_jaxpr/dot_general | solution.py:28
  94.9 4.4 %convolution_add_fusion.2 = f32[2048,256]{1,0:T(8,128)} fusion(f32[2048,256]{1,0:T(8,128)} %get-tuple-element.100, bf16[2048,256]{1,0:T(8,128)(2,1)S(1)} %get-tuple-element.109, pred[]{:T(512)S(6)} %compare.3, bf16[8,512,256]{2,1,0:T(8,128)(2,1)} %get-tuple-element.110, s32[]{:T(128)S(6)} %copy.6, bf16[8,512,256]{2,1,0:T(8,128)(2,1)} %get-tuple-element.108), kind=kOutput, calls=%fused_computation.2.clone.1 | convolution fusion | flops 1078984704 | bytes 5768704 | tf_op jit(solution)/shard_map/while/body/eval_jaxpr/dot_general | solution.py:28
  99.3 4.4 %convolution_add_fusion.2 = f32[2048,256]{1,0:T(8,128)} fusion(f32[2048,256]{1,0:T(8,128)} %get-tuple-element.100, bf16[2048,256]{1,0:T(8,128)(2,1)S(1)} %get-tuple-element.109, pred[]{:T(512)S(6)} %compare.3, bf16[8,512,256]{2,1,0:T(8,128)(2,1)} %get-tuple-element.110, s32[]{:T(128)S(6)} %copy.6, bf16[8,512,256]{2,1,0:T(8,128)(2,1)} %get-tuple-element.108), kind=kOutput, calls=%fused_computation.2.clone.1 | convolution fusion | flops 1078984704 | bytes 5768704 | tf_op jit(solution)/shard_map/while/body/eval_jaxpr/dot_general | solution.py:28
  103.8 0.1 dynamic_slice.10
  103.9 42.9 %reduce-scatter.2.cloned.1.call-done = f32[512,256]{1,0:T(8,128)} async-done(((f32[2048,256]{1,0:T(8,128)}), f32[512,256]{1,0:T(8,128)}) %reduce-scatter.2.cloned.1.call-update) | async-done | bytes 524304 | tf_op jit(solution)/shard_map/reduce_scatter | solution.py:46
  146.8 2.0 %broadcast_multiply_fusion = f32[512,256]{1,0:T(8,128)} fusion(f32[512,256]{1,0:T(8,128)} %reduce-scatter.2.cloned.1.call-done, f32[512]{0:T(512)S(1)} %dynamic_slice.10), kind=kLoop, calls=%fused_computation.13 | loop fusion | flops 131072 | bytes 1050624 | tf_op jit(solution)/shard_map/mul | solution.py:47
  (9 shorter events, 0.0 us)
Async XLA Ops:
  6.5 5.3 %copy-start = (f32[2048,256]{1,0:T(8,128)S(1)}, f32[2048,256]{1,0:T(8,128)}, u32[]{:S(2)}) copy-start(f32[2048,256]{1,0:T(8,128)} %param.5) | copy-start | bytes 6291460
  6.5 33.0 %all-gather.5.cloned.1.call-start = ((), (), s32[]{:S(2)}) async-start(), calls=%async_computation.2 | async-start | bytes 2359296 | tf_op jit(solution)/shard_map/all_gather | solution.py:41
  7.3 61.9 %all-gather.3.cloned.1.call-start = ((), (), s32[]{:S(2)}) async-start(), calls=%async_computation.1 | async-start | bytes 2359296 | tf_op jit(solution)/shard_map/all_gather | solution.py:40
  11.8 135.0 %reduce-scatter.2.cloned.1.call-start = ((), (), s32[]{:S(2)}) async-start(), calls=%async_computation.3 | async-start | bytes 2621440 | tf_op jit(solution)/shard_map/reduce_scatter | solution.py:46
Sparse Core Ops, SparseCore 0:
  9.2 30.2 all-gather.4
  41.4 27.7 all-gather.2
  103.9 42.8 reduce-scatter.1
where the time goes:
time: 157 us; the launch traced here: 155 us
  waiting for transfers between devices  99.2 us (63%)
  matrix products  34.6 us (22%)
  between operations  13.2 us (8%)
  other arithmetic  8.1 us (5%)
    reduce_scatter x1, waiting for transfers between devices, on_device(): own_rows = lax.psum_scatter(summed, 'dp', scatter_dimension=0, tiled=True)  42.9 us
    dot_general x8, matrix products, advance(): jnp.dot(localized, pair[1], preferred_element_type=jnp.float32)  34.6 us
    all_gather x1, waiting for transfers between devices, on_device(): lax.all_gather(data_std, 'state', axis=0, tiled=True)  29.7 us
    all_gather x1, waiting for transfers between devices, on_device(): lax.all_gather(innovations, 'state', axis=0, tiled=True)  25.9 us
  transfers between devices with their start and end apart: 3, of which 3 were waited for; matrix products, arithmetic and copies ran while one was open for 4% of the time, Pallas kernels for 0%

commit v1 on v0

v1 whole, which is shorter than its diff:
```python
import functools

import jax
import jax.numpy as jnp
from jax import lax
from jax.experimental import pallas as pl
from jax.experimental.pallas import tpu as pltpu
from jax.sharding import PartitionSpec as P

MESH = pl.DeviceIdType.MESH
PIECES = 2


def standardize(values):
    members = values.shape[1]
    anomalies = values - jnp.mean(values, axis=1, keepdims=True)
    spread = jnp.sqrt(jnp.sum(anomalies * anomalies, axis=1, keepdims=True) / (members - 1) + 1e-06)
    return anomalies * (1.0 / spread), spread


def kernel(n_s, n_dp, state_in, data_in, innov_in, out_ref, state_raw, data_raw, sbuf, spread_buf,
           acc, dbuf, nbuf, rs_out, rs_in, local_sem, send_sem, recv_sem, rs_send_sem, rs_recv_sem):
    s = lax.axis_index("state")
    d = lax.axis_index("dp")
    rows, members = state_in.shape
    count = data_in.shape[0]
    half = count // 2
    outers = n_s // 4
    core, inner, outer = lax.rem(s, 2), lax.rem(lax.div(s, 2), 2), lax.div(s, 4)
    sib = s + 1 - 2 * core
    across = s + 2 - 4 * inner
    across_sib = sib + 2 - 4 * inner

    def other(base, k):
        return lax.rem(base + 4 * k, n_s)

    right, left = lax.rem(d + 1, n_dp), lax.rem(d + n_dp - 1, n_dp)

    load_data = [
        pltpu.make_async_copy(
            data_in.at[pl.ds(h * half, half)], data_raw.at[pl.ds(h * half, half)], local_sem.at[h])
        for h in range(2)
    ]
    load_innov = [
        pltpu.make_async_copy(
            innov_in.at[pl.ds(h * half, half)], nbuf.at[s, h], local_sem.at[2 + h])
        for h in range(2)
    ]
    load_state = pltpu.make_async_copy(state_in, state_raw, local_sem.at[4])
    for h in (1, 0):
        load_data[h].start()
    load_state.start()
    for h in range(2):
        load_innov[h].start()

    barrier = pltpu.get_barrier_semaphore()
    partners = [sib, across] + [other(s, k) for k in range(1, outers)]
    for p in partners:
        pl.semaphore_signal(barrier, inc=1, device_id={"state": p}, device_id_type=MESH)
    for p in (right, left):
        pl.semaphore_signal(barrier, inc=1, device_id={"dp": p}, device_id_type=MESH)
    pl.semaphore_wait(barrier, len(partners) + 2)

    sends = []

    def send(array, owner, h, dest, src=None):
        buf = (dbuf, nbuf)[array]
        copy = pltpu.make_async_remote_copy(
            src_ref=buf.at[owner, h] if src is None else src,
            dst_ref=buf.at[owner, h],
            send_sem=send_sem.at[len(sends)],
            recv_sem=recv_sem.at[array, owner, h],
            device_id={"state": dest},
            device_id_type=MESH,
        )
        copy.start()
        sends.append(copy)

    def arrived(array, owner, h):
        buf = (dbuf, nbuf)[array]
        pltpu.make_async_remote_copy(
            src_ref=buf.at[owner, h],
            dst_ref=buf.at[owner, h],
            send_sem=send_sem.at[0],
            recv_sem=recv_sem.at[array, owner, h],
            device_id={"state": across},
            device_id_type=MESH,
        ).wait_recv()

    outer_ks = list(range(1, outers))

    def send_innov(h, dests):
        for dest in dests:
            send(1, s, h, dest, src=innov_in.at[pl.ds(h * half, half)])

    outer_devs = [other(s, k) for k in outer_ks]
    send_innov(1, [across])
    send_innov(0, outer_devs + [sib])

    for h in (1, 0):
        load_data[h].wait()
        std, _ = standardize(data_raw[pl.ds(h * half, half), :])
        dbuf[s, h] = std.T.astype(jnp.bfloat16)
    send(0, s, 1, across)
    for dest in outer_devs:
        send(0, s, 0, dest)
    send(0, s, 0, sib)
    send_innov(0, [across])
    send_innov(1, outer_devs + [sib])
    send(0, s, 0, across)
    for dest in outer_devs:
        send(0, s, 1, dest)
    send(0, s, 1, sib)

    load_state.wait()
    tile = rows // 8

    def state_tile(j, carry):
        at = pl.ds(pl.multiple_of(j * tile, tile), tile)
        std, spread = standardize(state_raw[at, :])
        sbuf[at, :] = std.astype(jnp.bfloat16)
        spread_buf[at, :] = spread
        return carry

    lax.fori_loop(0, 8, state_tile, 0)

    def partial(at, units):
        x = sbuf[at, :]
        total = None
        for owner, h in units:
            correl = jnp.dot(x, dbuf[owner, h], preferred_element_type=jnp.float32)
            localized = (correl * correl * correl).astype(jnp.bfloat16)
            term = jnp.dot(localized, nbuf[owner, h], preferred_element_type=jnp.float32)
            total = term if total is None else total + term
        return total

    def compute(units, first=False):
        def step(j, carry):
            at = pl.ds(pl.multiple_of(j * tile, tile), tile)
            total = partial(at, units)
            acc[at, :] = total if first else acc[at, :] + total
            return carry

        lax.fori_loop(0, 8, step, 0)

    def both(owner, h):
        arrived(1, owner, h)
        arrived(0, owner, h)

    def take(owner, h, onward):
        for array in (1, 0):
            arrived(array, owner, h)
            for dest in onward:
                send(array, owner, h, dest)

    for h in range(2):
        load_innov[h].wait()
    compute([(s, 0), (s, 1)], first=True)
    both(sib, 0)
    both(sib, 1)
    compute([(sib, 0), (sib, 1)])

    take(across, 1, outer_devs + [sib])
    for k in outer_ks:
        take(other(s, k), 0, [across, sib])
    compute([(across, 1)] + [(other(s, k), 0) for k in outer_ks])
    both(across_sib, 1)
    for k in outer_ks:
        both(other(sib, k), 0)
    take(across, 0, [sib])
    for k in outer_ks:
        take(other(s, k), 1, [sib])
    compute([(across_sib, 1)] + [(other(sib, k), 0) for k in outer_ks])
    compute([(across, 0)] + [(other(s, k), 1) for k in outer_ks])
    both(across_sib, 0)
    for k in outer_ks:
        both(other(sib, k), 1)
    compute([(across_sib, 0)] + [(other(sib, k), 1) for k in outer_ks])

    last_units = []
    for k in outer_ks:
        own_plane, sib_plane = other(across, k), other(across_sib, k)
        for h in range(2):
            take(own_plane, h, [sib])
        if k < outers - 1:
            compute([(own_plane, 0), (own_plane, 1)])
        for h in range(2):
            both(sib_plane, h)
        if k < outers - 1:
            compute([(sib_plane, 0), (sib_plane, 1)])
        else:
            last_units = [(own_plane, 0), (own_plane, 1), (sib_plane, 0), (sib_plane, 1)]

    target_rows = rows // n_dp
    ring_rows = target_rows // 2
    piece = ring_rows // PIECES
    scale = 1.0 / float(members - 1) ** 3

    def rs_copy(way, step, p):
        return pltpu.make_async_remote_copy(
            src_ref=rs_out.at[way, step, p],
            dst_ref=rs_in.at[way, step, p],
            send_sem=rs_send_sem.at[way, step, p],
            recv_sem=rs_recv_sem.at[way, step, p],
            device_id={"dp": (right, left)[way]},
            device_id_type=MESH,
        )

    for step in range(n_dp):
        for way in range(2):
            target = lax.rem(d + (n_dp - 1 - step if way == 0 else 1 + step), n_dp)
            base = target * target_rows + way * ring_rows
            at = pl.ds(pl.multiple_of(base, ring_rows), ring_rows)
            acc[at, :] += partial(at, last_units)
        for p in range(PIECES):
            for way in range(2):
                target = lax.rem(d + (n_dp - 1 - step if way == 0 else 1 + step), n_dp)
                base = target * target_rows + way * ring_rows + p * piece
                at = pl.ds(pl.multiple_of(base, piece), piece)
                value = acc[at, :]
                if step > 0:
                    rs_copy(way, step - 1, p).wait_recv()
                    value = value + rs_in[way, step - 1, p].astype(jnp.float32)
                if step < n_dp - 1:
                    rs_out[way, step, p] = value.astype(jnp.bfloat16)
                    rs_copy(way, step, p).start()
                else:
                    out_ref[pl.ds(way * ring_rows + p * piece, piece), :] = (
                        value * (spread_buf[at, :] * scale))

    for copy in sends:
        copy.wait_send()
    for step in range(n_dp - 1):
        for way in range(2):
            for p in range(PIECES):
                rs_copy(way, step, p).wait_send()


def on_device(n_s, n_dp, state_ensemble, predicted_data, innovations):
    rows, members = state_ensemble.shape
    count = predicted_data.shape[0]
    half = count // 2
    outers = n_s // 4
    n_sends = 4 * (n_s // 2) + 4 + 2 * (outers - 1) + 6 * (outers - 1)
    ring = (2, n_dp - 1, PIECES, rows // n_dp // 2 // PIECES, members)
    any_spec = pl.BlockSpec(memory_space=pl.ANY)
    return pl.pallas_call(
        functools.partial(kernel, n_s, n_dp),
        out_shape=jax.ShapeDtypeStruct((rows // n_dp, members), jnp.float32),
        in_specs=[any_spec] * 3,
        out_specs=pl.BlockSpec(memory_space=pltpu.VMEM),
        scratch_shapes=[
            pltpu.VMEM((rows, members), jnp.float32),
            pltpu.VMEM((count, members), jnp.float32),
            pltpu.VMEM((rows, members), jnp.bfloat16),
            pltpu.VMEM((rows, 1), jnp.float32),
            pltpu.VMEM((rows, members), jnp.float32),
            pltpu.VMEM((n_s, 2, members, half), jnp.bfloat16),
            pltpu.VMEM((n_s, 2, half, members), jnp.bfloat16),
            pltpu.VMEM(ring, jnp.bfloat16),
            pltpu.VMEM(ring, jnp.bfloat16),
            pltpu.SemaphoreType.DMA((5,)),
            pltpu.SemaphoreType.DMA((n_sends,)),
            pltpu.SemaphoreType.DMA((2, n_s, 2)),
            pltpu.SemaphoreType.DMA(ring[:3]),
            pltpu.SemaphoreType.DMA(ring[:3]),
        ],
        compiler_params=pltpu.CompilerParams(
            collective_id=0, has_side_effects=True, vmem_limit_bytes=48 * 1024 * 1024),
    )(state_ensemble, predicted_data, innovations)


def solution(mesh):
    in_specs = (P("state", None), P(("state", "dp"), None), P(("state", "dp"), None))
    out_specs = P(("state", "dp"), None)
    body = functools.partial(on_device, mesh.shape["state"], mesh.shape["dp"])
    return jax.shard_map(
        body, mesh=mesh, in_specs=in_specs, out_specs=out_specs, check_vma=False
    )
```

time: 157 us -> 56.8 us (0.36)
  waiting for transfers between devices: 99.2 us -> 0 us
  Pallas kernels: 0 us -> 52.2 us
  matrix products: 34.6 us -> 0 us
  between operations: 13.2 us -> 0.01 us
  other arithmetic: 8.1 us -> 0 us
  local copies, waits for them, and re-layouts: 0.08 us -> 4.38 us
    all_gather x2 -> x0, waiting for transfers between devices: 55.6 us -> none  [the longest x1 29.7 us: on_device(): lax.all_gather(data_std, 'state', axis=0, tiled=True)]
    pallas_call x0 -> x1, Pallas kernels: none -> 52.2 us  [on_device(): pl.pallas_call(functools.partial(kernel, n_s, n_dp), out_shape=jax.ShapeD...]
    reduce_scatter x1 -> x0, waiting for transfers between devices: 42.9 us -> none  [on_device(): own_rows = lax.psum_scatter(summed, 'dp', scatter_dimension=0, tiled=True)]
    dot_general x8 -> x0, matrix products: 34.6 us -> none  [advance(): jnp.dot(localized, pair[1], preferred_element_type=jnp.float32)]
    unnamed x2 -> x7, local copies, waits for them, and re-layouts: 0.01 us -> 4.38 us
    reduce_sum x4 -> x0, other arithmetic: 3.43 us -> none  [the longest x2 1.9 us: standardize(): jnp.sum(anomalies * anomalies, axis=1) / (members - 1) + 1e-06]
    convert_element_type x2 -> x0, other arithmetic: 2.67 us -> none  [standardize(): return ((anomalies / spread[:, None]).astype(jnp.bfloat16), spread)]
    mul x1 -> x0, other arithmetic: 1.97 us -> none  [on_device(): return own_spread[:, None] * own_rows]
  transfers between devices with their start and end apart: 3 -> 0, of which waited for: 3 -> 0; matrix products, arithmetic and copies ran while one was open for 4% -> 0% of each run, Pallas kernels for 0% -> 0%
where the time goes in v1:
time: 56.8 us; the launch traced here: 56.6 us
  Pallas kernels  52.2 us (92%)
  local copies, waits for them, and re-layouts  4.38 us (8%)
    pallas_call x1, Pallas kernels, on_device(): pl.pallas_call(functools.partial(kernel, n_s, n_dp), out_shape=jax.ShapeD...  52.2 us
    unnamed x7, local copies, waits for them, and re-layouts  4.38 us

profile of v1, /device:TPU:1, one launch (start us, length us, event | category | flops | bytes accessed | tf_op | source)
XLA Modules:
  0.0 56.6 jit_solution(1100660502765368814)
XLA Ops:
  0.0 0.0 copy-start
  0.0 1.6 %copy-done = f32[2048,256]{1,0:T(8,128)S(1)} copy-done((f32[2048,256]{1,0:T(8,128)S(1)}, f32[2048,256]{1,0:T(8,128)}, u32[]{:S(2)}) %copy-start) | copy-done | bytes 2097176
  1.6 0.0 copy-start.1
  1.6 1.0 %copy-done.1 = f32[512,256]{1,0:T(8,128)S(1)} copy-done((f32[512,256]{1,0:T(8,128)S(1)}, f32[512,256]{1,0:T(8,128)}, u32[]{:S(2)}) %copy-start.1) | copy-done | bytes 524312
  2.6 0.0 copy-start.2
  2.6 0.9 %copy-done.2 = bf16[512,256]{1,0:T(8,128)(2,1)S(1)} copy-done((bf16[512,256]{1,0:T(8,128)(2,1)S(1)}, bf16[512,256]{1,0:T(8,128)(2,1)}, u32[]{:S(2)}) %copy-start.2) | copy-done | bytes 262168
  3.6 52.2 %shard_map.37 = f32[512,256]{1,0:T(8,128)S(1)} custom-call(f32[2048,256]{1,0:T(8,128)S(1)} %copy-done, f32[512,256]{1,0:T(8,128)S(1)} %copy-done.1, bf16[512,256]{1,0:T(8,128)(2,1)S(1)} %copy-done.2), custom_call_target="tpu_custom_call" | custom-call | tf_op jit(solution)/shard_map/pallas_call | solution.py:247
  55.8 0.8 %copy.5 = f32[512,256]{1,0:T(8,128)} copy(f32[512,256]{1,0:T(8,128)S(1)} %shard_map.37) | data formatting | bytes 1048576
Async XLA Ops:
  0.0 1.6 %copy-start = (f32[2048,256]{1,0:T(8,128)S(1)}, f32[2048,256]{1,0:T(8,128)}, u32[]{:S(2)}) copy-start(f32[2048,256]{1,0:T(8,128)} %state_in.1) | copy-start | bytes 6291460
  1.6 1.0 %copy-start.1 = (f32[512,256]{1,0:T(8,128)S(1)}, f32[512,256]{1,0:T(8,128)}, u32[]{:S(2)}) copy-start(f32[512,256]{1,0:T(8,128)} %data_in.1) | copy-start | bytes 1572868
  2.6 0.9 %copy-start.2 = (bf16[512,256]{1,0:T(8,128)(2,1)S(1)}, bf16[512,256]{1,0:T(8,128)(2,1)}, u32[]{:S(2)}) copy-start(bf16[512,256]{1,0:T(8,128)(2,1)} %innov_in.1) | copy-start | bytes 786436

commit v2 on v1

--- a/solution.py
+++ b/solution.py
@@ -8,6 +8,7 @@
 from jax.sharding import PartitionSpec as P
 
 MESH = pl.DeviceIdType.MESH
+WIDE_STEPS = 2
 PIECES = 2
 
 
@@ -114,6 +115,7 @@
 
     load_state.wait()
     tile = rows // 8
+    wide = rows // WIDE_STEPS
 
     def state_tile(j, carry):
         at = pl.ds(pl.multiple_of(j * tile, tile), tile)
@@ -124,8 +126,7 @@
 
     lax.fori_loop(0, 8, state_tile, 0)
 
-    def partial(at, units):
-        x = sbuf[at, :]
+    def partial(x, units):
         total = None
         for owner, h in units:
             correl = jnp.dot(x, dbuf[owner, h], preferred_element_type=jnp.float32)
@@ -136,12 +137,12 @@
 
     def compute(units, first=False):
         def step(j, carry):
-            at = pl.ds(pl.multiple_of(j * tile, tile), tile)
-            total = partial(at, units)
+            at = pl.ds(pl.multiple_of(j * wide, wide), wide)
+            total = partial(sbuf[at, :], units)
             acc[at, :] = total if first else acc[at, :] + total
             return carry
 
-        lax.fori_loop(0, 8, step, 0)
+        lax.fori_loop(0, WIDE_STEPS, step, 0)
 
     def both(owner, h):
         arrived(1, owner, h)
@@ -207,11 +208,14 @@
         )
 
     for step in range(n_dp):
+        ats = []
         for way in range(2):
             target = lax.rem(d + (n_dp - 1 - step if way == 0 else 1 + step), n_dp)
             base = target * target_rows + way * ring_rows
-            at = pl.ds(pl.multiple_of(base, ring_rows), ring_rows)
-            acc[at, :] += partial(at, last_units)
+            ats.append(pl.ds(pl.multiple_of(base, ring_rows), ring_rows))
+        total = partial(jnp.concatenate([sbuf[at, :] for at in ats], axis=0), last_units)
+        for way in range(2):
+            acc[ats[way], :] += total[way * ring_rows:(way + 1) * ring_rows]
         for p in range(PIECES):
             for way in range(2):
                 target = lax.rem(d + (n_dp - 1 - step if way == 0 else 1 + step), n_dp)
@@ -243,7 +247,7 @@
     outers = n_s // 4
     n_sends = 4 * (n_s // 2) + 4 + 2 * (outers - 1) + 6 * (outers - 1)
     ring = (2, n_dp - 1, PIECES, rows // n_dp // 2 // PIECES, members)
-    any_spec = pl.BlockSpec(memory_space=pl.ANY)
+    any_spec = pl.BlockSpec(memory_space=pltpu.HBM)
     return pl.pallas_call(
         functools.partial(kernel, n_s, n_dp),
         out_shape=jax.ShapeDtypeStruct((rows // n_dp, members), jnp.float32),

time: 56.8 us -> 51.8 us (0.912)
  Pallas kernels: 52.2 us -> 47.2 us
    pallas_call x1, Pallas kernels: 52.2 us -> 47.2 us  [on_device(): pl.pallas_call(functools.partial(kernel, n_s, n_dp), out_shape=jax.ShapeD...]
where the time goes in v2:
time: 51.8 us; the launch traced here: 51.5 us
  Pallas kernels  47.2 us (91%)
  local copies, waits for them, and re-layouts  4.38 us (8%)
    pallas_call x1, Pallas kernels, on_device(): pl.pallas_call(functools.partial(kernel, n_s, n_dp), out_shape=jax.ShapeD...  47.2 us
    unnamed x7, local copies, waits for them, and re-layouts  4.38 us

profile of v2, /device:TPU:1, one launch (start us, length us, event | category | flops | bytes accessed | tf_op | source)
XLA Modules:
  0.0 51.5 jit_solution(840934239562469448)
XLA Ops:
  0.0 0.0 copy-start
  0.0 1.6 %copy-done = f32[2048,256]{1,0:T(8,128)S(1)} copy-done((f32[2048,256]{1,0:T(8,128)S(1)}, f32[2048,256]{1,0:T(8,128)}, u32[]{:S(2)}) %copy-start) | copy-done | bytes 2097176
  1.6 0.0 copy-start.1
  1.6 1.0 %copy-done.1 = f32[512,256]{1,0:T(8,128)S(1)} copy-done((f32[512,256]{1,0:T(8,128)S(1)}, f32[512,256]{1,0:T(8,128)}, u32[]{:S(2)}) %copy-start.1) | copy-done | bytes 524312
  2.6 0.0 copy-start.2
  2.6 0.9 %copy-done.2 = bf16[512,256]{1,0:T(8,128)(2,1)S(1)} copy-done((bf16[512,256]{1,0:T(8,128)(2,1)S(1)}, bf16[512,256]{1,0:T(8,128)(2,1)}, u32[]{:S(2)}) %copy-start.2) | copy-done | bytes 262168
  3.6 47.2 %shard_map.37 = f32[512,256]{1,0:T(8,128)S(1)} custom-call(f32[2048,256]{1,0:T(8,128)S(1)} %copy-done, f32[512,256]{1,0:T(8,128)S(1)} %copy-done.1, bf16[512,256]{1,0:T(8,128)(2,1)S(1)} %copy-done.2), custom_call_target="tpu_custom_call" | custom-call | tf_op jit(solution)/shard_map/pallas_call | solution.py:251
  50.8 0.8 %copy.5 = f32[512,256]{1,0:T(8,128)} copy(f32[512,256]{1,0:T(8,128)S(1)} %shard_map.37) | data formatting | bytes 1048576
Async XLA Ops:
  0.0 1.6 %copy-start = (f32[2048,256]{1,0:T(8,128)S(1)}, f32[2048,256]{1,0:T(8,128)}, u32[]{:S(2)}) copy-start(f32[2048,256]{1,0:T(8,128)} %state_in.1) | copy-start | bytes 6291460
  1.6 1.0 %copy-start.1 = (f32[512,256]{1,0:T(8,128)S(1)}, f32[512,256]{1,0:T(8,128)}, u32[]{:S(2)}) copy-start(f32[512,256]{1,0:T(8,128)} %data_in.1) | copy-start | bytes 1572868
  2.6 0.9 %copy-start.2 = (bf16[512,256]{1,0:T(8,128)(2,1)S(1)}, bf16[512,256]{1,0:T(8,128)(2,1)}, u32[]{:S(2)}) copy-start(bf16[512,256]{1,0:T(8,128)(2,1)} %innov_in.1) | copy-start | bytes 786436

commit v3 on v2

--- a/solution.py
+++ b/solution.py
@@ -8,7 +8,7 @@
 from jax.sharding import PartitionSpec as P
 
 MESH = pl.DeviceIdType.MESH
-WIDE_STEPS = 2
+WIDE_STEPS = 1
 PIECES = 2
 
 
@@ -270,7 +270,7 @@
             pltpu.SemaphoreType.DMA(ring[:3]),
         ],
         compiler_params=pltpu.CompilerParams(
-            collective_id=0, has_side_effects=True, vmem_limit_bytes=48 * 1024 * 1024),
+            collective_id=0, has_side_effects=True, vmem_limit_bytes=67043328),
     )(state_ensemble, predicted_data, innovations)
 
 

time: 51.8 us -> 48.2 us (0.931)
  local copies, waits for them, and re-layouts: 4.38 us -> 1.87 us
  Pallas kernels: 47.2 us -> 46.2 us
    unnamed x7 -> x1, local copies, waits for them, and re-layouts: 4.38 us -> 1.87 us
    pallas_call x1, Pallas kernels: 47.2 us -> 46.2 us  [on_device(): pl.pallas_call(functools.partial(kernel, n_s, n_dp), out_shape=jax.ShapeD...]
where the time goes in v3:
time: 48.2 us; the launch traced here: 48.1 us
  Pallas kernels  46.2 us (96%)
  local copies, waits for them, and re-layouts  1.87 us (4%)
    pallas_call x1, Pallas kernels, on_device(): pl.pallas_call(functools.partial(kernel, n_s, n_dp), out_shape=jax.ShapeD...  46.2 us
    unnamed x1, local copies, waits for them, and re-layouts  1.87 us

profile of v3, /device:TPU:1, one launch (start us, length us, event | category | flops | bytes accessed | tf_op | source)
XLA Modules:
  0.0 48.1 jit_solution(15060591381515964205)
XLA Ops:
  0.0 46.2 %shard_map.37 = f32[512,256]{1,0:T(8,128)} custom-call(f32[2048,256]{1,0:T(8,128)} %state_in.1, f32[512,256]{1,0:T(8,128)} %data_in.1, bf16[512,256]{1,0:T(8,128)(2,1)} %innov_in.1), custom_call_target="tpu_custom_call" | custom-call | tf_op jit(solution)/shard_map/pallas_call | solution.py:251
  46.2 1.9 %copy.5 = f32[512,256]{1,0:T(8,128)} copy(f32[512,256]{1,0:T(8,128)} %shard_map.37) | data formatting | bytes 1048576

commit v4 on v3

--- a/solution.py
+++ b/solution.py
@@ -185,12 +185,12 @@
             take(own_plane, h, [sib])
         if k < outers - 1:
             compute([(own_plane, 0), (own_plane, 1)])
-        for h in range(2):
-            both(sib_plane, h)
         if k < outers - 1:
+            for h in range(2):
+                both(sib_plane, h)
             compute([(sib_plane, 0), (sib_plane, 1)])
         else:
-            last_units = [(own_plane, 0), (own_plane, 1), (sib_plane, 0), (sib_plane, 1)]
+            last_units = [[(own_plane, 0), (own_plane, 1)], [(sib_plane, 0), (sib_plane, 1)]]
 
     target_rows = rows // n_dp
     ring_rows = target_rows // 2
@@ -213,7 +213,14 @@
             target = lax.rem(d + (n_dp - 1 - step if way == 0 else 1 + step), n_dp)
             base = target * target_rows + way * ring_rows
             ats.append(pl.ds(pl.multiple_of(base, ring_rows), ring_rows))
-        total = partial(jnp.concatenate([sbuf[at, :] for at in ats], axis=0), last_units)
+        x = jnp.concatenate([sbuf[at, :] for at in ats], axis=0)
+        if step == 0:
+            total = partial(x, last_units[0])
+            for owner, h in last_units[1]:
+                both(owner, h)
+            total = total + partial(x, last_units[1])
+        else:
+            total = partial(x, last_units[0] + last_units[1])
         for way in range(2):
             acc[ats[way], :] += total[way * ring_rows:(way + 1) * ring_rows]
         for p in range(PIECES):
@@ -270,8 +277,8 @@
             pltpu.SemaphoreType.DMA(ring[:3]),
         ],
         compiler_params=pltpu.CompilerParams(
-            collective_id=0, has_side_effects=True, vmem_limit_bytes=67043328),
-    )(state_ensemble, predicted_data, innovations)
+            collective_id=0, has_side_effects=True, vmem_limit_bytes=40000000),
+    )(*[pltpu.with_memory_space_constraint(x, pltpu.HBM) for x in (state_ensemble, predicted_data, innovations)])
 
 
 def solution(mesh):

time: 48.2 us -> 46.2 us (0.959)
  local copies, waits for them, and re-layouts: 1.87 us -> 0.8 us
  Pallas kernels: 46.2 us -> 45.2 us
    unnamed x1, local copies, waits for them, and re-layouts: 1.87 us -> 0.8 us
    pallas_call x1, Pallas kernels: 46.2 us -> 45.2 us  [on_device(): pl.pallas_call(functools.partial(kernel, n_s, n_dp), out_shape=jax.ShapeD...]
where the time goes in v4:
time: 46.2 us; the launch traced here: 46.1 us
  Pallas kernels  45.2 us (98%)
  local copies, waits for them, and re-layouts  0.8 us (2%)
    pallas_call x1, Pallas kernels, on_device(): pl.pallas_call(functools.partial(kernel, n_s, n_dp), out_shape=jax.ShapeD...  45.2 us

profile of v4, /device:TPU:1, one launch (start us, length us, event | category | flops | bytes accessed | tf_op | source)
XLA Modules:
  0.0 46.1 jit_solution(10317435731473023980)
XLA Ops:
  0.0 45.2 %shard_map.37 = f32[512,256]{1,0:T(8,128)S(1)} custom-call(f32[2048,256]{1,0:T(8,128)} %state_in.1, f32[512,256]{1,0:T(8,128)} %data_in.1, bf16[512,256]{1,0:T(8,128)(2,1)} %innov_in.1), custom_call_target="tpu_custom_call" | custom-call | tf_op jit(solution)/shard_map/pallas_call | solution.py:258
  45.3 0.8 %copy.5 = f32[512,256]{1,0:T(8,128)} copy(f32[512,256]{1,0:T(8,128)S(1)} %shard_map.37) | data formatting | bytes 1048576

commit v5 on v4

--- a/solution.py
+++ b/solution.py
@@ -207,27 +207,33 @@
             device_id_type=MESH,
         )
 
-    for step in range(n_dp):
-        ats = []
-        for way in range(2):
-            target = lax.rem(d + (n_dp - 1 - step if way == 0 else 1 + step), n_dp)
-            base = target * target_rows + way * ring_rows
-            ats.append(pl.ds(pl.multiple_of(base, ring_rows), ring_rows))
+    def ring_at(way, step, first, size):
+        target = lax.rem(d + (n_dp - 1 - step if way == 0 else 1 + step), n_dp)
+        base = target * target_rows + way * ring_rows + first
+        return pl.ds(pl.multiple_of(base, size), size)
+
+    def last_blocks(step, first, size):
+        ats = [ring_at(way, step, first, size) for way in range(2)]
         x = jnp.concatenate([sbuf[at, :] for at in ats], axis=0)
         if step == 0:
             total = partial(x, last_units[0])
-            for owner, h in last_units[1]:
-                both(owner, h)
+            if first == 0:
+                for owner, h in last_units[1]:
+                    both(owner, h)
             total = total + partial(x, last_units[1])
         else:
             total = partial(x, last_units[0] + last_units[1])
         for way in range(2):
-            acc[ats[way], :] += total[way * ring_rows:(way + 1) * ring_rows]
+            acc[ats[way], :] += total[way * size:(way + 1) * size]
+
+    for step in range(n_dp):
+        if step > 0:
+            last_blocks(step, 0, ring_rows)
         for p in range(PIECES):
+            if step == 0:
+                last_blocks(step, p * piece, piece)
             for way in range(2):
-                target = lax.rem(d + (n_dp - 1 - step if way == 0 else 1 + step), n_dp)
-                base = target * target_rows + way * ring_rows + p * piece
-                at = pl.ds(pl.multiple_of(base, piece), piece)
+                at = ring_at(way, step, p * piece, piece)
                 value = acc[at, :]
                 if step > 0:
                     rs_copy(way, step - 1, p).wait_recv()

time: 46.2 us -> 45.8 us (level)
  no operation moved by 1% of the time
where the time goes in v5:
time: 45.8 us; the launch traced here: 45.7 us
  Pallas kernels  44.9 us (98%)
  local copies, waits for them, and re-layouts  0.8 us (2%)
    pallas_call x1, Pallas kernels, on_device(): pl.pallas_call(functools.partial(kernel, n_s, n_dp), out_shape=jax.ShapeD...  44.9 us

profile of v5, /device:TPU:1, one launch (start us, length us, event | category | flops | bytes accessed | tf_op | source)
XLA Modules:
  0.0 45.7 jit_solution(14850870881069365478)
XLA Ops:
  0.0 44.9 %shard_map.37 = f32[512,256]{1,0:T(8,128)S(1)} custom-call(f32[2048,256]{1,0:T(8,128)} %state_in.1, f32[512,256]{1,0:T(8,128)} %data_in.1, bf16[512,256]{1,0:T(8,128)(2,1)} %innov_in.1), custom_call_target="tpu_custom_call" | custom-call | tf_op jit(solution)/shard_map/pallas_call | solution.py:264
  44.9 0.8 %copy.5 = f32[512,256]{1,0:T(8,128)} copy(f32[512,256]{1,0:T(8,128)S(1)} %shard_map.37) | data formatting | bytes 1048576
